TPU v7x, 128 devices: a whole 4x4x4 slice. The times are simulated.
128 devices in a mesh: row: 8 (over z, core), col: 8 (over x, y_hi), depth: 2 (over y_lo).
Axes of the slice: x: 4, y: 4 (y_hi: 2, y_lo: 2; y = y_hi * 2 + y_lo), z: 4, core: 2. Of those that a mesh axis runs over, the one named last changes fastest.
Arguments:
- amplitudes: bfloat16 [616, 616, 1024], P('col', 'row', 'depth'), may hold values from -6 to 6
- ladder_ints: bfloat16 [616, 616, 1024], P('col', 'row', 'depth'), may hold values from -0.013671875 to 0.013671875
- cycle_ints: bfloat16 [616, 32, 2048], P('row', None, 'col'), may hold values from -0.0625 to 0.0625
- ladder_source: float32 [1024, 1024], P(('row', 'col'), 'depth'), may hold values from -6 to 6
- cycle_source: float32 [616, 32, 2048], P('col', 'depth', 'row'), may hold values from -6 to 6
- occ_energy: float32 [32], replicated, may hold values from -2 to -0.4
- virt_energy: float32 [616], replicated, may hold values from 0.2 to 3
- pair_energy: float32 [1024], P(('row', 'col')), may hold values from 0.4 to 6
- slice_energy: float32 [64], replicated, may hold values from 0.2 to 3
Outputs:
- ladder_new: float32 [1024, 1024], P(('row', 'col'), 'depth')
- cycle_new: float32 [616, 32, 2048], P('col', 'depth', 'row')
All inputs are finite; a program needn't handle non-finite values.
Results may differ from a plain program's by a relative error of at most 0.0003.
Values may be sent and summed in bfloat16 or wider, within the bound.
No kernel may reach another device: no remote copies, remote signals or barrier semaphores. Data moves between devices by JAX's collectives and lax.ppermute only.
A program may use at most 128 MiB of HBM per device.

v0:
```python
import jax
import jax.numpy as jnp
from jax import lax
from jax.sharding import PartitionSpec as P


def body(
    amplitudes,
    ladder_ints,
    cycle_ints,
    ladder_source,
    cycle_source,
    occ_energy,
    virt_energy,
    pair_energy,
    slice_energy,
):
    virt_col, virt_row, pair_occ = amplitudes.shape
    occ_all = occ_energy.shape[0]
    occ_dev = pair_occ // occ_all
    inner = virt_col * virt_row
    flat_amp = amplitudes.reshape(inner, pair_occ)
    piece = lax.all_gather(ladder_ints, "depth", axis=2, tiled=True)
    partial_sum = lax.dot_general(
        piece.reshape(inner, piece.shape[2]),
        flat_amp,
        (((0,), (0,)), ((), ())),
        preferred_element_type=jnp.float32,
    )
    ladder_sum = lax.psum_scatter(partial_sum, ("row", "col"), scatter_dimension=0, tiled=True)
    occ_mine = lax.dynamic_slice_in_dim(occ_energy, lax.axis_index("depth") * occ_dev, occ_dev)
    occ_pairs = (occ_mine[:, None] + occ_energy[None, :]).reshape(pair_occ)
    ladder_den = occ_pairs[None, :] - pair_energy[:, None]
    ladder_new = (ladder_source + ladder_sum) / ladder_den
    slice_size = slice_energy.shape[0]
    cycle_amp = (
        amplitudes.reshape(virt_col, virt_row, occ_dev, occ_all)
        .transpose(0, 2, 1, 3)
        .reshape(virt_col * occ_dev, virt_row * occ_all)
    )
    piece = lax.all_gather(cycle_ints, "col", axis=2, tiled=True)
    cycle_part = jnp.dot(
        cycle_amp,
        piece.reshape(virt_row * occ_all, piece.shape[2]),
        preferred_element_type=jnp.float32,
    )
    cycle_part = cycle_part.reshape(virt_col, occ_dev, occ_all * slice_size)
    cycle_sum = lax.psum_scatter(cycle_part, "row", scatter_dimension=2, tiled=True)
    occ_share = cycle_sum.shape[2] // slice_size
    occ_rows = lax.dynamic_slice_in_dim(occ_energy, lax.axis_index("row") * occ_share, occ_share)
    virt_mine = lax.dynamic_slice_in_dim(virt_energy, lax.axis_index("col") * virt_col, virt_col)
    jb_part = (occ_rows[:, None] - slice_energy[None, :]).reshape(occ_share * slice_size)
    cycle_den = occ_mine[None, :, None] - virt_mine[:, None, None] + jb_part[None, None, :]
    cycle_new = (cycle_source + cycle_sum) / cycle_den
    return (ladder_new, cycle_new)


def solution(mesh):
    placed = (
        P("col", "row", "depth"),
        P("col", "row", "depth"),
        P("row", None, "col"),
        P(("row", "col"), "depth"),
        P("col", "depth", "row"),
        P(),
        P(),
        P(("row", "col")),
        P(),
    )
    return jax.shard_map(
        body,
        mesh=mesh,
        in_specs=placed,
        out_specs=(P(("row", "col"), "depth"), P("col", "depth", "row")),
        check_vma=False,
    )
```

profile of v0, /device:TPU:1, one launch (start us, length us, event | category | flops | bytes accessed | tf_op | source)
XLA Modules:
  0.0 716.0 jit_solution(5468249073596840638)
XLA Ops:
  7.2 0.0 copy-start
  7.2 0.0 all-gather.3.cloned.1.call-start
  7.2 0.7 all-gather.3.cloned.1.call-update
  7.9 0.0 all-gather.5.cloned.1.call-start
  8.0 0.5 copy-done
  8.5 1.8 copy.14
  10.2 0.0 all-gather.5.cloned.1.call-update
  10.2 0.0 reduce-scatter.3.cloned.1.call-start
  10.3 11.4 %copy.13 = bf16[77,77,512]{1,2,0:T(8,128)(2,1)} copy(bf16[77,77,512]{2,1,0:T(8,128)(2,1)} %param.9) | data formatting | bytes 12142592 | tf_op args[0]
  21.7 146.7 %all-gather.3.cloned.1.call-done = bf16[77,77,1024]{2,1,0:T(8,128)(2,1)} async-done(((bf16[77,77,512]{2,1,0:T(8,128)(2,1)}), bf16[77,77,1024]{2,1,0:T(8,128)(2,1)}) %all-gather.3.cloned.1.call-update) | async-done | bytes 12142608 | tf_op jit(solution)/shard_map/all_gather | solution.py:23
  168.3 12.8 %convolution_bitcast_fusion = f32[1024,512]{1,0:T(8,128)} fusion(bf16[77,77,1024]{2,1,0:T(8,128)(2,1)} %all-gather.3.cloned.1.call-done, bf16[77,77,512]{2,1,0:T(8,128)(2,1)} %param.9), kind=kOutput, calls=%fused_computation.4 | convolution fusion | flops 6217007104 | bytes 20311040 | tf_op jit(solution)/shard_map/dot_general | solution.py:24
  181.1 0.0 reduce-scatter.3.cloned.1.call-update
  181.1 0.0 reduce-scatter.5.cloned.1.call-start
  181.2 131.4 %all-gather.5.cloned.1.call-done = bf16[77,32,2048]{2,0,1:T(8,128)(2,1)} async-done(((bf16[77,32,256]{2,0,1:T(8,128)(2,1)}), bf16[77,32,2048]{2,0,1:T(8,128)(2,1)}) %all-gather.5.cloned.1.call-update) | async-done | bytes 10092560 | tf_op jit(solution)/shard_map/all_gather | solution.py:41
  312.5 34.6 %fusion.3 = f32[77,16,2048]{2,1,0:T(8,128)} fusion(bf16[77,32,2048]{2,0,1:T(8,128)(2,1)} %all-gather.5.cloned.1.call-done, bf16[77,16,77,32]{2,3,1,0:T(8,128)(2,1)} %bitcast.15), kind=kOutput, calls=%fused_computation.3 | convolution fusion | flops 12434014208 | bytes 26256384 | tf_op jit(solution)/shard_map/dot_general | solution.py:42
  347.2 0.0 copy-start.4
  347.2 0.0 copy-start.5
  347.2 0.0 copy-start.2
  347.2 0.0 copy-start.3
  347.2 0.0 copy-start.1
  347.2 0.0 reduce-scatter.5.cloned.1.call-update
  347.2 0.6 copy-done.4
  347.8 0.1 dynamic_slice.9
  347.9 0.1 broadcast_add_fusion
  348.0 0.1 add.57
  348.0 0.1 dynamic_slice.11
  348.1 0.0 copy-done.5
  348.1 0.1 broadcast_subtract_fusion.1
  348.2 0.1 sub.60
  348.3 0.8 dynamic_slice.10
  349.0 0.1 broadcast_subtract_fusion
  349.1 290.9 %reduce-scatter.3.cloned.1.call-done = f32[16,512]{1,0:T(8,128)} async-done(((f32[1024,512]{1,0:T(8,128)}), f32[16,512]{1,0:T(8,128)}) %reduce-scatter.3.cloned.1.call-update) | async-done | bytes 32784 | tf_op jit(solution)/shard_map/reduce_scatter | solution.py:30
  640.0 0.0 copy-done.2
  640.0 0.0 copy-done.3
  640.0 1.5 subtract_divide_fusion
  641.5 65.4 %reduce-scatter.5.cloned.1.call-done = f32[77,16,256]{2,1,0:T(8,128)} async-done(((f32[77,16,2048]{2,1,0:T(8,128)}), f32[77,16,256]{2,1,0:T(8,128)}) %reduce-scatter.5.cloned.1.call-update) | async-done | bytes 1261584 | tf_op jit(solution)/shard_map/reduce_scatter | solution.py:48
  706.9 0.0 copy-done.1
  706.9 2.6 add_divide_fusion
Async XLA Ops:
  7.2 1.3 copy-start
  7.2 161.2 %all-gather.3.cloned.1.call-start = ((), (), s32[]{:S(2)}) async-start(), calls=%async_computation.2 | async-start | bytes 18923520 | tf_op jit(solution)/shard_map/all_gather | solution.py:23
  7.9 304.6 %all-gather.5.cloned.1.call-start = ((), (), s32[]{:S(2)}) async-start(), calls=%async_computation.4 | async-start | bytes 11796480 | tf_op jit(solution)/shard_map/all_gather | solution.py:41
  10.2 629.8 %reduce-scatter.3.cloned.1.call-start = ((), (), s32[]{:S(2)}) async-start(), calls=%async_computation.3 | async-start | bytes 2129920 | tf_op jit(solution)/shard_map/reduce_scatter | solution.py:30
  181.1 525.8 %reduce-scatter.5.cloned.1.call-start = ((), (), s32[]{:S(2)}) async-start(), calls=%async_computation.5 | async-start | bytes 11354112 | tf_op jit(solution)/shard_map/reduce_scatter | solution.py:48
  347.2 0.7 copy-start.4
  347.2 1.0 copy-start.5
  347.2 292.8 %copy-start.2 = (f32[16,512]{1,0:T(8,128)S(1)}, f32[16,512]{1,0:T(8,128)}, u32[]{:S(2)}) copy-start(f32[16,512]{1,0:T(8,128)} %param.12) | copy-start | bytes 98308
  347.2 292.8 %copy-start.3 = (f32[16]{0:T(128)S(1)}, f32[16]{0:T(128)}, u32[]{:S(2)}) copy-start(f32[16]{0:T(128)} %param.16) | copy-start | bytes 196
  347.2 359.7 %copy-start.1 = (f32[77,16,256]{2,1,0:T(8,128)S(1)}, f32[77,16,256]{2,1,0:T(8,128)}, u32[]{:S(2)}) copy-start(f32[77,16,256]{2,1,0:T(8,128)} %param.13) | copy-start | bytes 3784708
Sparse Core Ops, SparseCore 0:
  9.7 158.6 all-gather.2
  170.5 141.9 all-gather.4
  314.9 325.0 reduce-scatter.2
  642.4 64.4 reduce-scatter.4
where the time goes:
time: 717 us; the launch traced here: 716 us
  waiting for transfers between devices  635 us (89%)
  matrix products  47.4 us (7%)
  local copies, waits for them, and re-layouts  15.3 us (2%)
  between operations  13.8 us (2%)
    reduce_scatter x1, waiting for transfers between devices, body(): lax.psum_scatter(partial_sum, ('row', 'col'), scatter_dimension=0, tiled=...  291 us
    all_gather x1, waiting for transfers between devices, body(): piece = lax.all_gather(ladder_ints, 'depth', axis=2, tiled=True)  147 us
    all_gather x1, waiting for transfers between devices, body(): piece = lax.all_gather(cycle_ints, 'col', axis=2, tiled=True)  131 us
    reduce_scatter x1, waiting for transfers between devices, body(): lax.psum_scatter(cycle_part, 'row', scatter_dimension=2, tiled=True)  65.4 us
    dot_general x1, matrix products, body(): jnp.dot(cycle_amp, piece.reshape(virt_row * occ_all, piece.shape[2]), pre...  34.6 us
  transfers between devices with their start and end apart: 4, of which 4 were waited for; matrix products, arithmetic and copies ran while one was open for 9% of the time, Pallas kernels for 0%

commit v1 on v0

--- a/solution.py
+++ b/solution.py
@@ -20,7 +20,9 @@
     occ_dev = pair_occ // occ_all
     inner = virt_col * virt_row
     flat_amp = amplitudes.reshape(inner, pair_occ)
-    piece = lax.all_gather(ladder_ints, "depth", axis=2, tiled=True)
+    piece = jnp.concatenate(
+        lax.all_to_all(jnp.stack([ladder_ints] * lax.axis_size("depth")), "depth", 0, 0), axis=2
+    )
     partial_sum = lax.dot_general(
         piece.reshape(inner, piece.shape[2]),
         flat_amp,

time: 717 us -> 678 us (0.946)
  waiting for transfers between devices: 635 us -> 537 us
  local copies, waits for them, and re-layouts: 15.3 us -> 57.1 us
  other arithmetic: 4.25 us -> 15.5 us
  starting transfers between devices: 0.16 us -> 9.3 us
    all_to_all x0 -> x1, waiting for transfers between devices: none -> 182 us  [body(): lax.all_to_all(jnp.stack([ladder_ints] * lax.axis_size('depth')), 'depth'...]
    all_gather x1 -> x0, waiting for transfers between devices: 147 us -> none  [body(): piece = lax.all_gather(ladder_ints, 'depth', axis=2, tiled=True)]
    all_gather x1, waiting for transfers between devices: 131 us -> 0.02 us  [body(): piece = lax.all_gather(cycle_ints, 'col', axis=2, tiled=True)]
    reshape x0 -> x2, local copies, waits for them, and re-layouts: none -> 27.1 us  [the longest x1 18.1 us: body(): jnp.concatenate(lax.all_to_all(jnp.stack([ladder_ints] * lax.axis_size('d...]
    unnamed x14 -> x18, local copies, waits for them, and re-layouts: 14.2 us -> 28.9 us
    another operation x0 -> x1, other arithmetic: none -> 11.2 us  [body(): jnp.stack([ladder_ints] * lax.axis_size('depth'))]
    all_to_all x0 -> x1, starting transfers between devices: none -> 9 us  [body(): lax.all_to_all(jnp.stack([ladder_ints] * lax.axis_size('depth')), 'depth'...]
  transfers between devices with their start and end apart: 4 -> 4, of which waited for: 4 -> 3; matrix products, arithmetic and copies ran while one was open for 9% -> 16% of each run, Pallas kernels for 0% -> 0%
where the time goes in v1:
time: 678 us; the launch traced here: 677 us
  waiting for transfers between devices  537 us (79%)
  local copies, waits for them, and re-layouts  57.1 us (8%)
  matrix products  42.6 us (6%)
  between operations  15.6 us (2%)
  other arithmetic  15.5 us (2%)
  starting transfers between devices  9.3 us (1%)
    reduce_scatter x1, waiting for transfers between devices, body(): lax.psum_scatter(partial_sum, ('row', 'col'), scatter_dimension=0, tiled=...  289 us
    all_to_all x1, waiting for transfers between devices, body(): lax.all_to_all(jnp.stack([ladder_ints] * lax.axis_size('depth')), 'depth'...  182 us
    reduce_scatter x1, waiting for transfers between devices, body(): lax.psum_scatter(cycle_part, 'row', scatter_dimension=2, tiled=True)  65.8 us
    dot_general x1, matrix products, body(): jnp.dot(cycle_amp, piece.reshape(virt_row * occ_all, piece.shape[2]), pre...  34.7 us
    unnamed x18, local copies, waits for them, and re-layouts  28.9 us
    reshape x1, local copies, waits for them, and re-layouts, body(): jnp.concatenate(lax.all_to_all(jnp.stack([ladder_ints] * lax.axis_size('d...  18.1 us
  transfers between devices with their start and end apart: 4, of which 3 were waited for; matrix products, arithmetic and copies ran while one was open for 16% of the time, Pallas kernels for 0%

profile of v1, /device:TPU:1, one launch (start us, length us, event | category | flops | bytes accessed | tf_op | source)
XLA Modules:
  0.0 676.9 jit_solution(7761072643385959673)
XLA Ops:
  8.0 0.0 all-gather.2.cloned.1.call-start
  8.0 3.1 copy.15
  11.1 0.0 all-gather.2.cloned.1.call-update
  11.1 11.2 %pad_maximum_fusion = bf16[2,77,77,512]{3,2,1,0:T(8,128)(2,1)} fusion(bf16[1,77,77,512]{3,2,1,0:T(8,128)(2,1)} %bitcast.23), kind=kLoop, calls=%fused_computation | loop fusion | flops 6071296 | bytes 18213888 | tf_op jit(solution)/shard_map/stack | solution.py:24
  22.3 9.0 %all-to-all-start = ((bf16[2,77,77,512]{3,2,1,0:T(8,128)(2,1)}), bf16[2,77,77,512]{3,2,1,0:T(8,128)(2,1)}, u32[]{:S(2)}, u32[]{:S(2)}) async-start(bf16[2,77,77,512]{3,2,1,0:T(8,128)(2,1)} %pad_maximum_fusion), calls=%async_computation | async-start | bytes 25231360 | tf_op jit(solution)/shard_map/all_to_all | solution.py:24
  31.3 0.0 reduce-scatter.3.cloned.1.call-start
  31.4 9.1 %reshape.84 = bf16[5929,512]{1,0:T(8,128)(2,1)} reshape(bf16[77,77,512]{2,1,0:T(8,128)(2,1)} %param.9) | data formatting | bytes 12142592 | tf_op jit(solution)/shard_map/reshape | solution.py:22
  40.5 11.4 %copy.14 = bf16[77,77,512]{1,2,0:T(8,128)(2,1)} copy(bf16[77,77,512]{2,1,0:T(8,128)(2,1)} %param.9) | data formatting | bytes 12142592 | tf_op args[0]
  51.8 181.9 %all-to-all-done = bf16[2,77,77,512]{3,2,1,0:T(8,128)(2,1)} async-done(((bf16[2,77,77,512]{3,2,1,0:T(8,128)(2,1)}), bf16[2,77,77,512]{3,2,1,0:T(8,128)(2,1)}, u32[]{:S(2)}, u32[]{:S(2)}) %all-to-all-start) | async-done | bytes 12142624 | tf_op jit(solution)/shard_map/all_to_all | solution.py:24
  233.7 18.1 %copy.13 = bf16[77,77,2,512]{3,2,1,0:T(2,128)(2,1)S(1)} copy(bf16[77,77,2,512]{3,1,0,2:T(8,128)(2,1)} %bitcast.1) | data formatting | bytes 24285184 | tf_op jit(solution)/shard_map/reshape | solution.py:23
  251.8 0.0 slice-start
  251.8 11.3 %pad.2 = bf16[5936,2,512]{2,1,0:T(2,128)(2,1)S(1)} pad(bf16[5929,2,512]{2,1,0:T(2,128)(2,1)S(1)} %bitcast.20, bf16[]{:T(256)} %constant.31), padding=0_7x0_0x0_0 | pad | bytes 24299522
  263.1 0.0 slice-start.1
  263.1 2.5 copy.18
  265.7 0.0 slice-done
  265.7 0.0 slice-done.1
  265.7 8.0 %fusion.8 = f32[1024,512]{1,0:T(8,128)} fusion(bf16[5929,1024]{1,0:T(8,128)(2,1)S(1)} %bitcast.21, bf16[5929,512]{1,0:T(8,128)(2,1)S(1)} %bitcast.25), kind=kOutput, calls=%fused_computation.10 | convolution fusion | flops 6217007104 | bytes 20311040 | tf_op jit(solution)/shard_map/dot_general | solution.py:26
  273.7 0.0 reduce-scatter.3.cloned.1.call-update
  273.7 0.2 reduce-scatter.5.cloned.1.call-start
  273.9 0.0 all-gather.2.cloned.1.call-done
  274.0 34.7 %fusion.3 = f32[77,16,2048]{2,1,0:T(8,128)} fusion(bf16[77,32,2048]{2,0,1:T(8,128)(2,1)} %all-gather.2.cloned.1.call-done, bf16[77,16,77,32]{2,3,1,0:T(8,128)(2,1)} %bitcast.22), kind=kOutput, calls=%fused_computation.4 | convolution fusion | flops 12434014208 | bytes 26256384 | tf_op jit(solution)/shard_map/dot_general | solution.py:44
  308.6 0.0 copy-start.3
  308.6 0.0 copy-start.4
  308.6 0.0 copy-start.1
  308.7 0.0 copy-start.2
  308.7 0.0 copy-start
  308.7 0.0 reduce-scatter.5.cloned.1.call-update
  308.7 0.6 copy-done.3
  309.3 0.1 dynamic_slice.9
  309.4 0.1 broadcast_add_fusion
  309.4 0.1 add.57
  309.5 0.1 dynamic_slice.11
  309.6 0.0 copy-done.4
  309.6 0.1 broadcast_subtract_fusion.1
  309.7 0.1 sub.60
  309.8 0.8 dynamic_slice.10
  310.5 0.1 broadcast_subtract_fusion
  310.6 289.1 %reduce-scatter.3.cloned.1.call-done = f32[16,512]{1,0:T(8,128)} async-done(((f32[1024,512]{1,0:T(8,128)}), f32[16,512]{1,0:T(8,128)}) %reduce-scatter.3.cloned.1.call-update) | async-done | bytes 32784 | tf_op jit(solution)/shard_map/reduce_scatter | solution.py:32
  599.7 0.0 copy-done.1
  599.7 0.0 copy-done.2
  599.7 1.5 subtract_divide_fusion
  601.1 65.8 %reduce-scatter.5.cloned.1.call-done = f32[77,16,256]{2,1,0:T(8,128)} async-done(((f32[77,16,2048]{2,1,0:T(8,128)}), f32[77,16,256]{2,1,0:T(8,128)}) %reduce-scatter.5.cloned.1.call-update) | async-done | bytes 1261584 | tf_op jit(solution)/shard_map/reduce_scatter | solution.py:50
  666.9 0.0 copy-done
  666.9 2.6 add_divide_fusion
  (1 shorter events, 0.0 us)
Async XLA Ops:
  8.0 266.0 %all-gather.2.cloned.1.call-start = ((), (), s32[]{:S(2)}) async-start(), calls=%async_computation.4 | async-start | bytes 11796480 | tf_op jit(solution)/shard_map/all_gather | solution.py:43
  22.3 211.4 %all-to-all-start = ((bf16[2,77,77,512]{3,2,1,0:T(8,128)(2,1)}), bf16[2,77,77,512]{3,2,1,0:T(8,128)(2,1)}, u32[]{:S(2)}, u32[]{:S(2)}) async-start(bf16[2,77,77,512]{3,2,1,0:T(8,128)(2,1)} %pad_maximum_fusion), calls=%async_computation | async-start | bytes 25231360 | tf_op jit(solution)/shard_map/all_to_all | solution.py:24
  31.3 568.3 %reduce-scatter.3.cloned.1.call-start = ((), (), s32[]{:S(2)}) async-start(), calls=%async_computation.3 | async-start | bytes 2129920 | tf_op jit(solution)/shard_map/reduce_scatter | solution.py:32
  251.8 13.9 %slice-start = ((s8[6078464]{0:T(1024)(128)(4,1)}), s8[4194304]{0:T(1024)(128)(4,1)S(1)}, s32[]{:S(2)}) async-start(s8[6078464]{0:T(1024)(128)(4,1)} %bitcast.24), calls=%async_computation.6 | async-start | bytes 8388608
  263.1 2.6 slice-start.1
  273.7 393.2 %reduce-scatter.5.cloned.1.call-start = ((), (), s32[]{:S(2)}) async-start(), calls=%async_computation.5 | async-start | bytes 11354112 | tf_op jit(solution)/shard_map/reduce_scatter | solution.py:50
  308.6 0.7 copy-start.3
  308.6 1.0 copy-start.4
  308.6 291.0 %copy-start.1 = (f32[16,512]{1,0:T(8,128)S(1)}, f32[16,512]{1,0:T(8,128)}, u32[]{:S(2)}) copy-start(f32[16,512]{1,0:T(8,128)} %param.12) | copy-start | bytes 98308
  308.7 291.0 %copy-start.2 = (f32[16]{0:T(128)S(1)}, f32[16]{0:T(128)}, u32[]{:S(2)}) copy-start(f32[16]{0:T(128)} %param.16) | copy-start | bytes 196
  308.7 358.2 %copy-start = (f32[77,16,256]{2,1,0:T(8,128)S(1)}, f32[77,16,256]{2,1,0:T(8,128)}, u32[]{:S(2)}) copy-start(f32[77,16,256]{2,1,0:T(8,128)} %param.13) | copy-start | bytes 3784708
Sparse Core Ops, SparseCore 0:
  11.2 205.5 all-gather.1
Sparse Core Ops, SparseCore 1:
  273.8 325.8 reduce-scatter.2
  602.1 64.7 reduce-scatter.4
